TPU v7x, 128 devices: a whole 4x4x4 slice. The times are simulated.
128 devices in a mesh: row: 8 (over x, core), col: 16 (over z, y).
Axes of the slice: x: 4, y: 4, z: 4, core: 2. Of those that a mesh axis runs over, the one named last changes fastest.
Arguments:
- surface_head: float32 [512, 4096], P('row', 'col'), may hold values from -6 to 6
- conduct_x: float32 [512, 4096], P('row', 'col'), may hold values from 0.01 to 0.1
- conduct_y: float32 [512, 4096], P('row', 'col'), may hold values from 0.01 to 0.1
- porosity: float32 [512, 4096], P('row', 'col'), may hold values from 0.45 to 1
- rainfall: float32 [512, 4096], P('row', 'col'), may hold values from 0.005 to 0.1
- pipe_head: float32 [32, 32768], P(None, ('row', 'col')), may hold values from -6 to 6
- pipe_class: int32 [32768], P(('row', 'col')), may hold values from 0 to 3
- pipe_up: int32 [32768], P(('row', 'col')), may hold values from 0 to 4095
- pipe_down: int32 [32768], P(('row', 'col')), may hold values from 0 to 4095
- pipe_matrices: float32 [4, 32, 32], replicated
- link_cell: int32 [128, 128, 64], P(('row', 'col')), may hold values from -1 to 16383, as said below
- link_node: int32 [128, 128, 64], P(None, ('row', 'col')), may hold values from -1 to 8191, as said below
- link_coef: float32 [128, 128, 64], P(None, ('row', 'col')), may hold values from 0.05 to 0.4
Outputs:
- surface_out: float32 [512, 4096], P('row', 'col')
- pipe_out: float32 [32, 32768], P(None, ('row', 'col'))
Inputs may be any that keep to these rules, and one draw needn't show every extreme that they name: `link_cell`: for each source tile and pipe owner the live slots come first; each is a cell of the source tile counted row by row; the other slots are -1. In every draw some tile sends 64 live slots to some owner. `link_node`: -1 exactly where link_cell is -1 at the same source tile, owner and slot; else a node of the owner's pipes, numbered node * 256 + pipe.
All inputs are finite; a program needn't handle non-finite values.
Results may differ from a plain program's by a relative error of at most 0.00015.
Values sent between devices are 32-bit elements; how exact they have to be, the bound alone decides.
No kernel may reach another device: no remote copies, remote signals or barrier semaphores. Data moves between devices by JAX's collectives and lax.ppermute only.
A program may use at most 64 MiB of HBM per device.

v0:
```python
import jax
import jax.numpy as jnp
from jax import lax
from jax.sharding import PartitionSpec as P

CLASSES = 4
SWEEPS = 4
STEPS = 3
boundary_gain = 0.5


def passed_along(block, axis, distance):
    devices = range(lax.axis_size(axis))
    route = [(i - distance, i) for i in devices if i - distance in devices]
    return lax.ppermute(block, axis, route)


def with_halo(block, sides, width):
    for axis, dim in sides:
        count = lax.axis_size(axis)
        forward = [(i, i + 1) for i in range(count - 1)]
        backward = [(target, source) for source, target in forward]
        low = lax.ppermute(
            lax.slice_in_dim(block, block.shape[dim] - width, None, axis=dim), axis, forward
        )
        high = lax.ppermute(lax.slice_in_dim(block, 0, width, axis=dim), axis, backward)
        block = jnp.concatenate([low, block, high], axis=dim)
    return block


def sweep_once(
    center, north, south, west, east, north_gain, south_gain, west_gain, east_gain, inverse, source
):
    change = (
        north_gain * (north - center)
        + south_gain * (south - center)
        + west_gain * (west - center)
        + east_gain * (east - center)
    )
    return center + change * inverse + source


def body(
    surface_head,
    conduct_x,
    conduct_y,
    porosity,
    rainfall,
    pipe_head,
    pipe_class,
    pipe_up,
    pipe_down,
    pipe_matrices,
    link_cell,
    link_node,
    link_coef,
):
    tile_rows, tile_cols = surface_head.shape
    inverse = 1.0 / porosity
    from_above = passed_along(conduct_x[-1:, :], "row", 1)
    north_gain = jnp.concatenate([from_above, conduct_x[:-1, :]], axis=0)
    from_left = passed_along(conduct_y[:, -1:], "col", 1)
    west_gain = jnp.concatenate([from_left, conduct_y[:, :-1]], axis=1)
    cell_index = link_cell[0]
    cell_live = cell_index >= 0
    cell_safe = jnp.where(cell_live, cell_index, 0)
    node_index = link_node[:, 0, :]
    node_live = node_index >= 0
    node_safe = jnp.where(node_live, node_index, 0)
    link_gain = link_coef[:, 0, :]
    inverse_flat = inverse.reshape(-1)
    surface = surface_head
    pipe_state = pipe_head
    for coupling_step in range(STEPS):
        for sweep_index in range(SWEEPS):
            padded = with_halo(surface, (("row", 0), ("col", 1)), 1)
            surface = sweep_once(
                surface,
                padded[:-2, 1:-1],
                padded[2:, 1:-1],
                padded[1:-1, :-2],
                padded[1:-1, 2:],
                north_gain,
                conduct_x,
                west_gain,
                conduct_y,
                inverse,
                rainfall,
            )
        surface_flat = surface.reshape(-1)
        sent_heads = jnp.where(cell_live, surface_flat[cell_safe], 0.0)
        pipe_flat = pipe_state.reshape(-1)
        pipe_at_slots = jnp.where(node_live, pipe_flat[node_safe], 0.0)
        arrived = lax.all_to_all(
            sent_heads, ("row", "col"), split_axis=0, concat_axis=0, tiled=True
        )
        manhole_flow = jnp.where(node_live, link_gain * (arrived - pipe_at_slots), 0.0)
        inflow = jnp.zeros_like(pipe_flat).at[node_safe].add(manhole_flow).reshape(pipe_state.shape)
        returned = lax.all_to_all(
            manhole_flow, ("row", "col"), split_axis=0, concat_axis=0, tiled=True
        )
        surface = (
            surface_flat.at[cell_safe]
            .add(-(returned * inverse_flat[cell_safe]))
            .reshape(tile_rows, tile_cols)
        )
        first_heads, last_heads = (
            lax.all_gather(pipe_state[0], "col", axis=0, tiled=True),
            lax.all_gather(pipe_state[-1], "col", axis=0, tiled=True),
        )
        balance = pipe_state + inflow
        balance = balance.at[0].add(boundary_gain * last_heads[pipe_up])
        balance = balance.at[-1].add(boundary_gain * first_heads[pipe_down])
        updated = jnp.zeros_like(pipe_state)
        for class_index in range(CLASSES):
            product = jnp.dot(
                pipe_matrices[class_index],
                balance,
                precision=lax.Precision.HIGHEST,
                preferred_element_type=jnp.float32,
            )
            updated = jnp.where(pipe_class[None, :] == class_index, product, updated)
        pipe_state = updated
    return (surface, pipe_state)


def solution(mesh):
    placed = (
        P("row", "col"),
        P("row", "col"),
        P("row", "col"),
        P("row", "col"),
        P("row", "col"),
        P(None, ("row", "col")),
        P(("row", "col")),
        P(("row", "col")),
        P(("row", "col")),
        P(),
        P(("row", "col"), None, None),
        P(None, ("row", "col"), None),
        P(None, ("row", "col"), None),
    )
    return jax.shard_map(
        body,
        mesh=mesh,
        in_specs=placed,
        out_specs=(P("row", "col"), P(None, ("row", "col"))),
        check_vma=False,
    )
```

profile of v0, /device:TPU:1, one launch (start us, length us, event | category | flops | bytes accessed | tf_op | source)
XLA Modules:
  0.0 1038.9 jit_solution(1538303368657251957)
XLA Ops:
  38.3 23.2 %all-gather = f32[1,4096]{1,0:T(1,128)S(1)} all-gather(f32[1,256]{1,0:T(1,128)S(1)} %get-tuple-element.133), channel_id=2, replica_groups=mesh['row'=8,'col'=16] {'col'}, dimensions={1}, use_global_device_ids=true | all-gather | bytes 17408 | tf_op jit(solution)/shard_map/all_gather | solution.py:109
  96.8 19.4 %all-gather.1 = f32[1,4096]{1,0:T(1,128)S(1)} all-gather(f32[1,256]{1,0:T(1,128)S(1)} %get-tuple-element.132), channel_id=3, replica_groups=mesh['row'=8,'col'=16] {'col'}, dimensions={1}, use_global_device_ids=true | all-gather | bytes 17408 | tf_op jit(solution)/shard_map/all_gather | solution.py:108
  118.2 45.5 %gather_fusion = f32[8192]{0:T(1024)S(1)} fusion(f32[16384]{0:T(1024)S(1)} %bitcast.123, s32[8192]{0:T(1024)S(1)} %broadcast_clamp_fusion.1), kind=kCustom, calls=%fused_computation | custom fusion | bytes 98304 | tf_op jit(solution)/shard_map/gather | solution.py:91
  164.5 12.9 %all-to-all-start = ((f32[128,1,64]{2,1,0:T(1,128)}), f32[128,1,64]{2,1,0:T(1,128)S(1)}, u32[]{:S(2)}, u32[]{:S(2)}) async-start(f32[128,1,64]{2,1,0:T(1,128)} %bitcast.2), calls=%async_computation | async-start | bytes 131072 | tf_op jit(solution)/shard_map/all_to_all | solution.py:94
  177.5 45.5 %gather_fusion.1 = f32[8192]{0:T(1024)S(1)} fusion(f32[8192]{0:T(1024)S(1)} %bitcast.130, s32[8192]{0:T(1024)S(1)} %broadcast_clamp_fusion), kind=kCustom, calls=%fused_computation.1 | custom fusion | bytes 98304 | tf_op jit(solution)/shard_map/gather | solution.py:93
  224.1 45.5 %gather_fusion.2 = f32[8192]{0:T(1024)S(1)} fusion(f32[16384]{0:T(1024)S(1)} %bitcast.132, s32[8192]{0:T(1024)S(1)} %broadcast_clamp_fusion.1), kind=kCustom, calls=%fused_computation.2 | custom fusion | bytes 98304 | tf_op jit(solution)/shard_map/gather | solution.py:104
  280.2 44.9 %scatter_custom_fusion.1 = f32[8192]{0:T(1024)S(1)} fusion(s32[8192]{0:T(1024)S(1)} %reshape.369, f32[8192]{0:T(1024)S(1)} %reshape.475, f32[]{:T(128)} %constant.152.clone.1), kind=kCustom, calls=%fused_computation.362 | custom fusion | flops 8192 | bytes 32772 | tf_op jit(solution)/shard_map/scatter-add | solution.py:98
  325.3 50.3 %scatter_fusion = f32[16384]{0:T(1024)S(1)} fusion(f32[16384]{0:T(1024)S(1)} %bitcast.124, s32[8192]{0:T(1024)S(1)} %reshape.465, f32[8192]{0:T(1024)S(1)} %reshape.467), kind=kCustom, calls=%fused_computation.13 | custom fusion | flops 8192 | bytes 131072 | tf_op jit(solution)/shard_map/scatter-add | solution.py:104
  383.4 9.8 collective-permute-start.20
  422.8 25.7 %all-gather.2 = f32[1,4096]{1,0:T(1,128)S(1)} all-gather(f32[1,256]{1,0:T(1,128)S(1)} %get-tuple-element.131), channel_id=4, replica_groups=mesh['row'=8,'col'=16] {'col'}, dimensions={1}, use_global_device_ids=true | all-gather | bytes 17408 | tf_op jit(solution)/shard_map/all_gather | solution.py:109
  468.7 17.2 %all-gather.3 = f32[1,4096]{1,0:T(1,128)S(1)} all-gather(f32[1,256]{1,0:T(1,128)S(1)} %get-tuple-element.130), channel_id=5, replica_groups=mesh['row'=8,'col'=16] {'col'}, dimensions={1}, use_global_device_ids=true | all-gather | bytes 17408 | tf_op jit(solution)/shard_map/all_gather | solution.py:108
  487.8 45.5 %gather_fusion.3 = f32[8192]{0:T(1024)S(1)} fusion(f32[16384]{0:T(1024)S(1)} %bitcast.125, s32[8192]{0:T(1024)S(1)} %broadcast_clamp_fusion.1), kind=kCustom, calls=%fused_computation.3 | custom fusion | bytes 98304 | tf_op jit(solution)/shard_map/gather | solution.py:91
  534.1 13.1 %all-to-all-start.2 = ((f32[128,1,64]{2,1,0:T(1,128)}), f32[128,1,64]{2,1,0:T(1,128)S(1)}, u32[]{:S(2)}, u32[]{:S(2)}) async-start(f32[128,1,64]{2,1,0:T(1,128)} %bitcast.9), calls=%async_computation.2 | async-start | bytes 131072 | tf_op jit(solution)/shard_map/all_to_all | solution.py:94
  547.2 45.5 %gather_fusion.6 = f32[8192]{0:T(1024)S(1)} fusion(f32[8192]{0:T(1024)S(1)} %bitcast.131, s32[8192]{0:T(1024)S(1)} %broadcast_clamp_fusion), kind=kCustom, calls=%fused_computation.6 | custom fusion | bytes 98304 | tf_op jit(solution)/shard_map/gather | solution.py:93
  603.4 44.9 %scatter_custom_fusion.3 = f32[8192]{0:T(1024)S(1)} fusion(s32[8192]{0:T(1024)S(1)} %reshape.369, f32[8192]{0:T(1024)S(1)} %reshape.491, f32[]{:T(128)} %constant.152.clone.1), kind=kCustom, calls=%fused_computation.360 | custom fusion | flops 8192 | bytes 32772 | tf_op jit(solution)/shard_map/scatter-add | solution.py:98
  648.6 50.3 %scatter_fusion.1 = f32[16384]{0:T(1024)S(1)} fusion(f32[16384]{0:T(1024)S(1)} %bitcast.126, s32[8192]{0:T(1024)S(1)} %reshape.465, f32[8192]{0:T(1024)S(1)} %reshape.483), kind=kCustom, calls=%fused_computation.15 | custom fusion | flops 8192 | bytes 131072 | tf_op jit(solution)/shard_map/scatter-add | solution.py:104
  746.0 25.7 %all-gather.4 = f32[1,4096]{1,0:T(1,128)S(1)} all-gather(f32[1,256]{1,0:T(1,128)S(1)} %get-tuple-element.129), channel_id=6, replica_groups=mesh['row'=8,'col'=16] {'col'}, dimensions={1}, use_global_device_ids=true | all-gather | bytes 17408 | tf_op jit(solution)/shard_map/all_gather | solution.py:109
  791.9 17.2 %all-gather.5 = f32[1,4096]{1,0:T(1,128)S(1)} all-gather(f32[1,256]{1,0:T(1,128)S(1)} %get-tuple-element.128), channel_id=7, replica_groups=mesh['row'=8,'col'=16] {'col'}, dimensions={1}, use_global_device_ids=true | all-gather | bytes 17408 | tf_op jit(solution)/shard_map/all_gather | solution.py:108
  811.0 45.5 %gather_fusion.7 = f32[8192]{0:T(1024)S(1)} fusion(f32[16384]{0:T(1024)S(1)} %bitcast.127, s32[8192]{0:T(1024)S(1)} %broadcast_clamp_fusion.1), kind=kCustom, calls=%fused_computation.7 | custom fusion | bytes 98304 | tf_op jit(solution)/shard_map/gather | solution.py:91
  857.3 13.1 %all-to-all-start.4 = ((f32[128,1,64]{2,1,0:T(1,128)}), f32[128,1,64]{2,1,0:T(1,128)S(1)}, u32[]{:S(2)}, u32[]{:S(2)}) async-start(f32[128,1,64]{2,1,0:T(1,128)} %bitcast.27), calls=%async_computation.4 | async-start | bytes 131072 | tf_op jit(solution)/shard_map/all_to_all | solution.py:94
  870.4 45.5 %gather_fusion.10 = f32[8192]{0:T(1024)S(1)} fusion(f32[8192]{0:T(1024)S(1)} %bitcast.129, s32[8192]{0:T(1024)S(1)} %broadcast_clamp_fusion), kind=kCustom, calls=%fused_computation.10 | custom fusion | bytes 98304 | tf_op jit(solution)/shard_map/gather | solution.py:93
  916.2 44.9 %scatter_custom_fusion.5 = f32[8192]{0:T(1024)S(1)} fusion(s32[8192]{0:T(1024)S(1)} %reshape.369, f32[8192]{0:T(1024)S(1)} %reshape.507, f32[]{:T(128)} %constant.152.clone.1), kind=kCustom, calls=%fused_computation.358 | custom fusion | flops 8192 | bytes 32772 | tf_op jit(solution)/shard_map/scatter-add | solution.py:98
  962.4 15.8 %all-to-all-start.5 = ((f32[128,1,64]{2,1,0:T(1,128)}), f32[128,1,64]{2,1,0:T(1,128)S(1)}, u32[]{:S(2)}, u32[]{:S(2)}) async-start(f32[128,1,64]{2,1,0:T(1,128)} %bitcast.35), calls=%async_computation.5 | async-start | bytes 131072 | tf_op jit(solution)/shard_map/all_to_all | solution.py:99
  988.0 50.3 %scatter_fusion.2 = f32[16384]{0:T(1024)S(1)} fusion(f32[16384]{0:T(1024)S(1)} %bitcast.128, s32[8192]{0:T(1024)S(1)} %reshape.465, f32[8192]{0:T(1024)S(1)} %reshape.499), kind=kCustom, calls=%fused_computation.17 | custom fusion | flops 8192 | bytes 131072 | tf_op jit(solution)/shard_map/scatter-add | solution.py:104
  (283 shorter events, 239.3 us)
Async XLA Ops:
  1.4 17.1 %collective-permute-start.2 = (f32[1,256]{1,0:T(1,128)S(1)}, f32[1,256]{1,0:T(1,128)S(1)}, u32[]{:S(2)}, u32[]{:S(2)}) collective-permute-start(f32[1,256]{1,0:T(1,128)S(1)} %get-tuple-element.127), channel_id=1, source_target_pairs={{16,0},{32,16},{48,32},{64,48},{80,64},{96,80},{112,96},{17,1},{33... | collective-permute-start | bytes 3080 | tf_op jit(solution)/shard_map/ppermute | solution.py:26
  4.7 13.8 %collective-permute-start.1 = (f32[1,256]{1,0:T(1,128)S(1)}, f32[1,256]{1,0:T(1,128)S(1)}, u32[]{:S(2)}, u32[]{:S(2)}) collective-permute-start(f32[1,256]{1,0:T(1,128)S(1)} %get-tuple-element.126), channel_id=1, source_target_pairs={{0,16},{16,32},{32,48},{48,64},{64,80},{80,96},{96,112},{1,17},{17... | collective-permute-start | bytes 3080 | tf_op jit(solution)/shard_map/ppermute | solution.py:23
  8.5 15.5 %collective-permute-start = (f32[1,256]{1,0:T(1,128)S(1)}, f32[1,256]{1,0:T(1,128)S(1)}, u32[]{:S(2)}, u32[]{:S(2)}) collective-permute-start(f32[1,256]{1,0:T(1,128)S(1)} %slice.500), channel_id=1, source_target_pairs={{0,16},{16,32},{32,48},{48,64},{64,80},{80,96},{96,112},{1,17},{17... | collective-permute-start | bytes 3080 | tf_op jit(solution)/shard_map/ppermute | solution.py:15
  32.4 30.8 %collective-permute-start.9 = (f32[66,1]{1,0:T(8,128)S(1)}, f32[66,1]{1,0:T(8,128)S(1)}, u32[]{:S(2)}, u32[]{:S(2)}) collective-permute-start(f32[66,1]{1,0:T(8,128)S(1)} %get-tuple-element.101), channel_id=1, source_target_pairs={{1,0},{2,1},{3,2},{4,3},{5,4},{6,5},{7,6},{8,7},{9,8},{10,9},{11,1... | collective-permute-start | bytes 800 | tf_op jit(solution)/shard_map/ppermute | solution.py:26
  33.7 29.5 %collective-permute-start.8 = (f32[66,1]{1,0:T(8,128)S(1)}, f32[66,1]{1,0:T(8,128)S(1)}, u32[]{:S(2)}, u32[]{:S(2)}) collective-permute-start(f32[66,1]{1,0:T(8,128)S(1)} %get-tuple-element.100), channel_id=1, source_target_pairs={{0,1},{1,2},{2,3},{3,4},{4,5},{5,6},{6,7},{7,8},{8,9},{9,10},{10,1... | collective-permute-start | bytes 800 | tf_op jit(solution)/shard_map/ppermute | solution.py:23
  63.3 12.2 %collective-permute-start.11 = (f32[1,256]{1,0:T(1,128)S(1)}, f32[1,256]{1,0:T(1,128)S(1)}, u32[]{:S(2)}, u32[]{:S(2)}) collective-permute-start(f32[1,256]{1,0:T(1,128)S(1)} %get-tuple-element.123), channel_id=1, source_target_pairs={{16,0},{32,16},{48,32},{64,48},{80,64},{96,80},{112,96},{17,1},{33... | collective-permute-start | bytes 3080 | tf_op jit(solution)/shard_map/ppermute | solution.py:26
  90.9 27.1 %collective-permute-start.17 = (f32[66,1]{1,0:T(8,128)S(1)}, f32[66,1]{1,0:T(8,128)S(1)}, u32[]{:S(2)}, u32[]{:S(2)}) collective-permute-start(f32[66,1]{1,0:T(8,128)S(1)} %get-tuple-element.97), channel_id=1, source_target_pairs={{1,0},{2,1},{3,2},{4,3},{5,4},{6,5},{7,6},{8,7},{9,8},{10,9},{11,1... | collective-permute-start | bytes 800 | tf_op jit(solution)/shard_map/ppermute | solution.py:26
  92.2 25.8 %collective-permute-start.16 = (f32[66,1]{1,0:T(8,128)S(1)}, f32[66,1]{1,0:T(8,128)S(1)}, u32[]{:S(2)}, u32[]{:S(2)}) collective-permute-start(f32[66,1]{1,0:T(8,128)S(1)} %get-tuple-element.96), channel_id=1, source_target_pairs={{0,1},{1,2},{2,3},{3,4},{4,5},{5,6},{6,7},{7,8},{8,9},{9,10},{10,1... | collective-permute-start | bytes 800 | tf_op jit(solution)/shard_map/ppermute | solution.py:23
  164.5 105.2 %all-to-all-start = ((f32[128,1,64]{2,1,0:T(1,128)}), f32[128,1,64]{2,1,0:T(1,128)S(1)}, u32[]{:S(2)}, u32[]{:S(2)}) async-start(f32[128,1,64]{2,1,0:T(1,128)} %bitcast.2), calls=%async_computation | async-start | bytes 131072 | tf_op jit(solution)/shard_map/all_to_all | solution.py:94
  270.3 54.9 %all-to-all-start.1 = ((f32[128,1,64]{2,1,0:T(1,128)}), f32[128,1,64]{2,1,0:T(1,128)S(1)}, u32[]{:S(2)}, u32[]{:S(2)}) async-start(f32[128,1,64]{2,1,0:T(1,128)} %bitcast.5), calls=%async_computation.1 | async-start | bytes 131072 | tf_op jit(solution)/shard_map/all_to_all | solution.py:99
  416.9 33.3 %collective-permute-start.29 = (f32[66,1]{1,0:T(8,128)S(1)}, f32[66,1]{1,0:T(8,128)S(1)}, u32[]{:S(2)}, u32[]{:S(2)}) collective-permute-start(f32[66,1]{1,0:T(8,128)S(1)} %get-tuple-element.91), channel_id=1, source_target_pairs={{1,0},{2,1},{3,2},{4,3},{5,4},{6,5},{7,6},{8,7},{9,8},{10,9},{11,1... | collective-permute-start | bytes 800 | tf_op jit(solution)/shard_map/ppermute | solution.py:26
  418.2 32.0 %collective-permute-start.28 = (f32[66,1]{1,0:T(8,128)S(1)}, f32[66,1]{1,0:T(8,128)S(1)}, u32[]{:S(2)}, u32[]{:S(2)}) collective-permute-start(f32[66,1]{1,0:T(8,128)S(1)} %get-tuple-element.90), channel_id=1, source_target_pairs={{0,1},{1,2},{2,3},{3,4},{4,5},{5,6},{6,7},{7,8},{8,9},{9,10},{10,1... | collective-permute-start | bytes 800 | tf_op jit(solution)/shard_map/ppermute | solution.py:23
  450.4 12.2 %collective-permute-start.31 = (f32[1,256]{1,0:T(1,128)S(1)}, f32[1,256]{1,0:T(1,128)S(1)}, u32[]{:S(2)}, u32[]{:S(2)}) collective-permute-start(f32[1,256]{1,0:T(1,128)S(1)} %get-tuple-element.113), channel_id=1, source_target_pairs={{16,0},{32,16},{48,32},{64,48},{80,64},{96,80},{112,96},{17,1},{33... | collective-permute-start | bytes 3080 | tf_op jit(solution)/shard_map/ppermute | solution.py:26
  463.4 24.2 %collective-permute-start.33 = (f32[66,1]{1,0:T(8,128)S(1)}, f32[66,1]{1,0:T(8,128)S(1)}, u32[]{:S(2)}, u32[]{:S(2)}) collective-permute-start(f32[66,1]{1,0:T(8,128)S(1)} %get-tuple-element.89), channel_id=1, source_target_pairs={{1,0},{2,1},{3,2},{4,3},{5,4},{6,5},{7,6},{8,7},{9,8},{10,9},{11,1... | collective-permute-start | bytes 800 | tf_op jit(solution)/shard_map/ppermute | solution.py:26
  464.7 22.9 %collective-permute-start.32 = (f32[66,1]{1,0:T(8,128)S(1)}, f32[66,1]{1,0:T(8,128)S(1)}, u32[]{:S(2)}, u32[]{:S(2)}) collective-permute-start(f32[66,1]{1,0:T(8,128)S(1)} %get-tuple-element.88), channel_id=1, source_target_pairs={{0,1},{1,2},{2,3},{3,4},{4,5},{5,6},{6,7},{7,8},{8,9},{9,10},{10,1... | collective-permute-start | bytes 800 | tf_op jit(solution)/shard_map/ppermute | solution.py:23
  534.1 58.8 %all-to-all-start.2 = ((f32[128,1,64]{2,1,0:T(1,128)}), f32[128,1,64]{2,1,0:T(1,128)S(1)}, u32[]{:S(2)}, u32[]{:S(2)}) async-start(f32[128,1,64]{2,1,0:T(1,128)} %bitcast.9), calls=%async_computation.2 | async-start | bytes 131072 | tf_op jit(solution)/shard_map/all_to_all | solution.py:94
  593.5 54.9 %all-to-all-start.3 = ((f32[128,1,64]{2,1,0:T(1,128)}), f32[128,1,64]{2,1,0:T(1,128)S(1)}, u32[]{:S(2)}, u32[]{:S(2)}) async-start(f32[128,1,64]{2,1,0:T(1,128)} %bitcast.23), calls=%async_computation.3 | async-start | bytes 131072 | tf_op jit(solution)/shard_map/all_to_all | solution.py:99
  740.2 33.3 %collective-permute-start.45 = (f32[66,1]{1,0:T(8,128)S(1)}, f32[66,1]{1,0:T(8,128)S(1)}, u32[]{:S(2)}, u32[]{:S(2)}) collective-permute-start(f32[66,1]{1,0:T(8,128)S(1)} %get-tuple-element.83), channel_id=1, source_target_pairs={{1,0},{2,1},{3,2},{4,3},{5,4},{6,5},{7,6},{8,7},{9,8},{10,9},{11,1... | collective-permute-start | bytes 800 | tf_op jit(solution)/shard_map/ppermute | solution.py:26
  741.5 32.0 %collective-permute-start.44 = (f32[66,1]{1,0:T(8,128)S(1)}, f32[66,1]{1,0:T(8,128)S(1)}, u32[]{:S(2)}, u32[]{:S(2)}) collective-permute-start(f32[66,1]{1,0:T(8,128)S(1)} %get-tuple-element.82), channel_id=1, source_target_pairs={{0,1},{1,2},{2,3},{3,4},{4,5},{5,6},{6,7},{7,8},{8,9},{9,10},{10,1... | collective-permute-start | bytes 800 | tf_op jit(solution)/shard_map/ppermute | solution.py:23
  773.6 12.2 %collective-permute-start.47 = (f32[1,256]{1,0:T(1,128)S(1)}, f32[1,256]{1,0:T(1,128)S(1)}, u32[]{:S(2)}, u32[]{:S(2)}) collective-permute-start(f32[1,256]{1,0:T(1,128)S(1)} %get-tuple-element.105), channel_id=1, source_target_pairs={{16,0},{32,16},{48,32},{64,48},{80,64},{96,80},{112,96},{17,1},{33... | collective-permute-start | bytes 3080 | tf_op jit(solution)/shard_map/ppermute | solution.py:26
  786.6 24.2 %collective-permute-start.49 = (f32[66,1]{1,0:T(8,128)S(1)}, f32[66,1]{1,0:T(8,128)S(1)}, u32[]{:S(2)}, u32[]{:S(2)}) collective-permute-start(f32[66,1]{1,0:T(8,128)S(1)} %get-tuple-element.81), channel_id=1, source_target_pairs={{1,0},{2,1},{3,2},{4,3},{5,4},{6,5},{7,6},{8,7},{9,8},{10,9},{11,1... | collective-permute-start | bytes 800 | tf_op jit(solution)/shard_map/ppermute | solution.py:26
  787.9 22.9 %collective-permute-start.48 = (f32[66,1]{1,0:T(8,128)S(1)}, f32[66,1]{1,0:T(8,128)S(1)}, u32[]{:S(2)}, u32[]{:S(2)}) collective-permute-start(f32[66,1]{1,0:T(8,128)S(1)} %get-tuple-element.80), channel_id=1, source_target_pairs={{0,1},{1,2},{2,3},{3,4},{4,5},{5,6},{6,7},{7,8},{8,9},{9,10},{10,1... | collective-permute-start | bytes 800 | tf_op jit(solution)/shard_map/ppermute | solution.py:23
  857.3 58.8 %all-to-all-start.4 = ((f32[128,1,64]{2,1,0:T(1,128)}), f32[128,1,64]{2,1,0:T(1,128)S(1)}, u32[]{:S(2)}, u32[]{:S(2)}) async-start(f32[128,1,64]{2,1,0:T(1,128)} %bitcast.27), calls=%async_computation.4 | async-start | bytes 131072 | tf_op jit(solution)/shard_map/all_to_all | solution.py:94
  962.4 25.5 %all-to-all-start.5 = ((f32[128,1,64]{2,1,0:T(1,128)}), f32[128,1,64]{2,1,0:T(1,128)S(1)}, u32[]{:S(2)}, u32[]{:S(2)}) async-start(f32[128,1,64]{2,1,0:T(1,128)} %bitcast.35), calls=%async_computation.5 | async-start | bytes 131072 | tf_op jit(solution)/shard_map/all_to_all | solution.py:99
  (45 other events, 312.4 us)
where the time goes:
time: 1040 us
  local copies, waits for them, and re-layouts  339 us (33%)
  other arithmetic  291 us (28%)
  starting transfers between devices  254 us (24%)
  blocking collectives  128 us (12%)
  waiting for transfers between devices  21.3 us (2%)
    scatter-add x3, other arithmetic, body(): surface = surface_flat.at[cell_safe].add(-(returned * inverse_flat[cell_s...  151 us
    gather x9, local copies, waits for them, and re-layouts, body(): pipe_at_slots = jnp.where(node_live, pipe_flat[node_safe], 0.0)  137 us
    gather x6, local copies, waits for them, and re-layouts, body(): sent_heads = jnp.where(cell_live, surface_flat[cell_safe], 0.0)  137 us
    scatter-add x3, other arithmetic, body(): jnp.zeros_like(pipe_flat).at[node_safe].add(manhole_flow)  135 us
    ppermute x24, starting transfers between devices, with_halo(): lax.ppermute(lax.slice_in_dim(block, block.shape[dim] - width, None, axis...  118 us
    all_gather x3, blocking collectives, body(): lax.all_gather(pipe_state[-1], 'col', axis=0, tiled=True)  74.5 us
    ppermute x24, starting transfers between devices, with_halo(): lax.ppermute(lax.slice_in_dim(block, 0, width, axis=dim), axis, backward)  56 us
    all_gather x3, blocking collectives, body(): lax.all_gather(pipe_state[0], 'col', axis=0, tiled=True)  53.8 us
  transfers between devices with their start and end apart: 56, of which 18 were waited for; matrix products, arithmetic and copies ran while one was open for 28% of the time, Pallas kernels for 0%

commit v1 on v0

--- a/solution.py
+++ b/solution.py
@@ -105,7 +105,10 @@
             .reshape(tile_rows, tile_cols)
         )
         first_heads, last_heads = (
-            lax.all_gather(pipe_state[0], "col", axis=0, tiled=True),
+            jnp.concatenate(
+                lax.all_to_all(jnp.stack([pipe_state[0]] * lax.axis_size("col")), "col", 0, 0),
+                axis=0,
+            ),
             lax.all_gather(pipe_state[-1], "col", axis=0, tiled=True),
         )
         balance = pipe_state + inflow

time: 1040 us -> 1010 us (0.971)
  blocking collectives: 128 us -> 74.2 us
  waiting for transfers between devices: 21.3 us -> 48.3 us
    all_gather x3 -> x0, blocking collectives: 53.8 us -> none  [body(): lax.all_gather(pipe_state[0], 'col', axis=0, tiled=True)]
    all_to_all x3, waiting for transfers between devices: 0.01 us -> 27.4 us  [body(): lax.all_to_all(sent_heads, ('row', 'col'), split_axis=0, concat_axis=0, t...]
    all_to_all x3, starting transfers between devices: 35.3 us -> 18.4 us  [body(): lax.all_to_all(manhole_flow, ('row', 'col'), split_axis=0, concat_axis=0,...]
    all_to_all x0 -> x3, starting transfers between devices: none -> 15 us  [body(): lax.all_to_all(jnp.stack([pipe_state[0]] * lax.axis_size('col')), 'col',...]
  transfers between devices with their start and end apart: 56 -> 59, of which waited for: 18 -> 20; matrix products, arithmetic and copies ran while one was open for 28% -> 34% of each run, Pallas kernels for 0% -> 0%
where the time goes in v1:
time: 1010 us; the launch traced here: 1000 us
  local copies, waits for them, and re-layouts  340 us (34%)
  other arithmetic  291 us (29%)
  starting transfers between devices  244 us (24%)
  blocking collectives  74.2 us (7%)
  waiting for transfers between devices  48.3 us (5%)
    scatter-add x3, other arithmetic, body(): surface = surface_flat.at[cell_safe].add(-(returned * inverse_flat[cell_s...  151 us
    gather x9, local copies, waits for them, and re-layouts, body(): pipe_at_slots = jnp.where(node_live, pipe_flat[node_safe], 0.0)  137 us
    gather x6, local copies, waits for them, and re-layouts, body(): sent_heads = jnp.where(cell_live, surface_flat[cell_safe], 0.0)  137 us
    scatter-add x3, other arithmetic, body(): jnp.zeros_like(pipe_flat).at[node_safe].add(manhole_flow)  135 us
    ppermute x24, starting transfers between devices, with_halo(): lax.ppermute(lax.slice_in_dim(block, block.shape[dim] - width, None, axis...  118 us
    all_gather x3, blocking collectives, body(): lax.all_gather(pipe_state[-1], 'col', axis=0, tiled=True)  74.2 us
    ppermute x24, starting transfers between devices, with_halo(): lax.ppermute(lax.slice_in_dim(block, 0, width, axis=dim), axis, backward)  56.2 us
    gather x2, local copies, waits for them, and re-layouts, body(): inverse_flat[cell_safe]  45.6 us
  transfers between devices with their start and end apart: 59, of which 20 were waited for; matrix products, arithmetic and copies ran while one was open for 34% of the time, Pallas kernels for 0%

profile of v1, /device:TPU:1, one launch (start us, length us, event | category | flops | bytes accessed | tf_op | source)
XLA Modules:
  0.0 1003.0 jit_solution(121059017126330213)
XLA Ops:
  46.2 22.8 %all-gather = f32[1,4096]{1,0:T(1,128)S(1)} all-gather(f32[1,256]{1,0:T(1,128)S(1)} %get-tuple-element.133), channel_id=2, replica_groups=mesh['row'=8,'col'=16] {'col'}, dimensions={1}, use_global_device_ids=true | all-gather | bytes 17408 | tf_op jit(solution)/shard_map/all_gather | solution.py:112
  97.8 45.5 %gather_fusion.1 = f32[8192]{0:T(1024)S(1)} fusion(f32[8192]{0:T(1024)S(1)} %bitcast.133, s32[8192]{0:T(1024)S(1)} %broadcast_clamp_fusion), kind=kCustom, calls=%fused_computation.1 | custom fusion | bytes 98304 | tf_op jit(solution)/shard_map/gather | solution.py:93
  150.3 45.5 %gather_fusion.2 = f32[8192]{0:T(1024)S(1)} fusion(f32[16384]{0:T(1024)S(1)} %bitcast.135, s32[8192]{0:T(1024)S(1)} %broadcast_clamp_fusion.1), kind=kCustom, calls=%fused_computation.2 | custom fusion | bytes 98304 | tf_op jit(solution)/shard_map/gather | solution.py:104
  196.1 45.5 %gather_fusion = f32[8192]{0:T(1024)S(1)} fusion(f32[16384]{0:T(1024)S(1)} %bitcast.126, s32[8192]{0:T(1024)S(1)} %broadcast_clamp_fusion.1), kind=kCustom, calls=%fused_computation | custom fusion | bytes 98304 | tf_op jit(solution)/shard_map/gather | solution.py:91
  265.8 44.9 %scatter_custom_fusion.1 = f32[8192]{0:T(1024)S(1)} fusion(s32[8192]{0:T(1024)S(1)} %reshape.405, f32[8192]{0:T(1024)S(1)} %reshape.511, f32[]{:T(128)} %constant.152.clone.1), kind=kCustom, calls=%fused_computation.362 | custom fusion | flops 8192 | bytes 32772 | tf_op jit(solution)/shard_map/scatter-add | solution.py:98
  311.0 50.3 %scatter_fusion = f32[16384]{0:T(1024)S(1)} fusion(f32[16384]{0:T(1024)S(1)} %bitcast.127, s32[8192]{0:T(1024)S(1)} %reshape.501, f32[8192]{0:T(1024)S(1)} %reshape.503), kind=kCustom, calls=%fused_computation.13 | custom fusion | flops 8192 | bytes 131072 | tf_op jit(solution)/shard_map/scatter-add | solution.py:104
  369.0 9.8 collective-permute-start.20
  408.4 25.7 %all-gather.1 = f32[1,4096]{1,0:T(1,128)S(1)} all-gather(f32[1,256]{1,0:T(1,128)S(1)} %get-tuple-element.131), channel_id=3, replica_groups=mesh['row'=8,'col'=16] {'col'}, dimensions={1}, use_global_device_ids=true | all-gather | bytes 17408 | tf_op jit(solution)/shard_map/all_gather | solution.py:112
  448.2 45.5 %gather_fusion.6 = f32[8192]{0:T(1024)S(1)} fusion(f32[8192]{0:T(1024)S(1)} %bitcast.134, s32[8192]{0:T(1024)S(1)} %broadcast_clamp_fusion), kind=kCustom, calls=%fused_computation.6 | custom fusion | bytes 98304 | tf_op jit(solution)/shard_map/gather | solution.py:93
  506.6 45.5 %gather_fusion.3 = f32[8192]{0:T(1024)S(1)} fusion(f32[16384]{0:T(1024)S(1)} %bitcast.128, s32[8192]{0:T(1024)S(1)} %broadcast_clamp_fusion.1), kind=kCustom, calls=%fused_computation.3 | custom fusion | bytes 98304 | tf_op jit(solution)/shard_map/gather | solution.py:91
  552.9 10.8 %all-to-all-start.2 = ((f32[128,1,64]{2,1,0:T(1,128)}), f32[128,1,64]{2,1,0:T(1,128)S(1)}, u32[]{:S(2)}, u32[]{:S(2)}) async-start(f32[128,1,64]{2,1,0:T(1,128)} %bitcast.9), calls=%async_computation.2 | async-start | bytes 131072 | tf_op jit(solution)/shard_map/all_to_all | solution.py:94
  563.7 9.7 all-to-all-done.2
  578.5 44.9 %scatter_custom_fusion.3 = f32[8192]{0:T(1024)S(1)} fusion(s32[8192]{0:T(1024)S(1)} %reshape.405, f32[8192]{0:T(1024)S(1)} %reshape.527, f32[]{:T(128)} %constant.152.clone.1), kind=kCustom, calls=%fused_computation.360 | custom fusion | flops 8192 | bytes 32772 | tf_op jit(solution)/shard_map/scatter-add | solution.py:98
  623.6 50.3 %scatter_fusion.1 = f32[16384]{0:T(1024)S(1)} fusion(f32[16384]{0:T(1024)S(1)} %bitcast.129, s32[8192]{0:T(1024)S(1)} %reshape.501, f32[8192]{0:T(1024)S(1)} %reshape.519), kind=kCustom, calls=%fused_computation.15 | custom fusion | flops 8192 | bytes 131072 | tf_op jit(solution)/shard_map/scatter-add | solution.py:104
  681.6 9.8 collective-permute-start.36
  721.1 25.7 %all-gather.2 = f32[1,4096]{1,0:T(1,128)S(1)} all-gather(f32[1,256]{1,0:T(1,128)S(1)} %get-tuple-element.129), channel_id=4, replica_groups=mesh['row'=8,'col'=16] {'col'}, dimensions={1}, use_global_device_ids=true | all-gather | bytes 17408 | tf_op jit(solution)/shard_map/all_gather | solution.py:112
  760.9 45.5 %gather_fusion.10 = f32[8192]{0:T(1024)S(1)} fusion(f32[8192]{0:T(1024)S(1)} %bitcast.132, s32[8192]{0:T(1024)S(1)} %broadcast_clamp_fusion), kind=kCustom, calls=%fused_computation.10 | custom fusion | bytes 98304 | tf_op jit(solution)/shard_map/gather | solution.py:93
  819.3 45.5 %gather_fusion.7 = f32[8192]{0:T(1024)S(1)} fusion(f32[16384]{0:T(1024)S(1)} %bitcast.130, s32[8192]{0:T(1024)S(1)} %broadcast_clamp_fusion.1), kind=kCustom, calls=%fused_computation.7 | custom fusion | bytes 98304 | tf_op jit(solution)/shard_map/gather | solution.py:91
  865.5 10.8 %all-to-all-start.5 = ((f32[128,1,64]{2,1,0:T(1,128)}), f32[128,1,64]{2,1,0:T(1,128)S(1)}, u32[]{:S(2)}, u32[]{:S(2)}) async-start(f32[128,1,64]{2,1,0:T(1,128)} %bitcast.28), calls=%async_computation.5 | async-start | bytes 131072 | tf_op jit(solution)/shard_map/all_to_all | solution.py:94
  876.4 9.7 all-to-all-done.5
  886.2 44.9 %scatter_custom_fusion.5 = f32[8192]{0:T(1024)S(1)} fusion(s32[8192]{0:T(1024)S(1)} %reshape.405, f32[8192]{0:T(1024)S(1)} %reshape.543, f32[]{:T(128)} %constant.152.clone.1), kind=kCustom, calls=%fused_computation.358 | custom fusion | flops 8192 | bytes 32772 | tf_op jit(solution)/shard_map/scatter-add | solution.py:98
  932.4 9.8 all-to-all-start.7
  943.0 8.9 all-to-all-done.7
  952.0 50.3 %scatter_fusion.2 = f32[16384]{0:T(1024)S(1)} fusion(f32[16384]{0:T(1024)S(1)} %bitcast.131, s32[8192]{0:T(1024)S(1)} %reshape.501, f32[8192]{0:T(1024)S(1)} %reshape.535), kind=kCustom, calls=%fused_computation.17 | custom fusion | flops 8192 | bytes 131072 | tf_op jit(solution)/shard_map/scatter-add | solution.py:104
  (289 shorter events, 242.7 us)
Async XLA Ops:
  1.4 24.6 %collective-permute-start.2 = (f32[1,256]{1,0:T(1,128)S(1)}, f32[1,256]{1,0:T(1,128)S(1)}, u32[]{:S(2)}, u32[]{:S(2)}) collective-permute-start(f32[1,256]{1,0:T(1,128)S(1)} %get-tuple-element.127), channel_id=1, source_target_pairs={{16,0},{32,16},{48,32},{64,48},{80,64},{96,80},{112,96},{17,1},{33... | collective-permute-start | bytes 3080 | tf_op jit(solution)/shard_map/ppermute | solution.py:26
  4.7 21.3 %collective-permute-start.1 = (f32[1,256]{1,0:T(1,128)S(1)}, f32[1,256]{1,0:T(1,128)S(1)}, u32[]{:S(2)}, u32[]{:S(2)}) collective-permute-start(f32[1,256]{1,0:T(1,128)S(1)} %get-tuple-element.126), channel_id=1, source_target_pairs={{0,16},{16,32},{32,48},{48,64},{64,80},{80,96},{96,112},{1,17},{17... | collective-permute-start | bytes 3080 | tf_op jit(solution)/shard_map/ppermute | solution.py:23
  8.5 23.2 %collective-permute-start = (f32[1,256]{1,0:T(1,128)S(1)}, f32[1,256]{1,0:T(1,128)S(1)}, u32[]{:S(2)}, u32[]{:S(2)}) collective-permute-start(f32[1,256]{1,0:T(1,128)S(1)} %slice.506), channel_id=1, source_target_pairs={{0,16},{16,32},{32,48},{48,64},{64,80},{80,96},{96,112},{1,17},{17... | collective-permute-start | bytes 3080 | tf_op jit(solution)/shard_map/ppermute | solution.py:15
  11.9 19.8 %collective-permute-start.3 = (f32[64,1]{1,0:T(8,128)S(1)}, f32[64,1]{1,0:T(8,128)S(1)}, u32[]{:S(2)}, u32[]{:S(2)}) collective-permute-start(f32[64,1]{1,0:T(8,128)S(1)} %slice.512), channel_id=1, source_target_pairs={{0,1},{1,2},{2,3},{3,4},{4,5},{5,6},{6,7},{7,8},{8,9},{9,10},{10,1... | collective-permute-start | bytes 776 | tf_op jit(solution)/shard_map/ppermute | solution.py:15
  15.8 226.5 %all-to-all-start.3 = ((f32[16,1,256]{2,1,0:T(1,128)}), f32[16,1,256]{2,1,0:T(1,128)S(1)}, u32[]{:S(2)}, u32[]{:S(2)}) async-start(f32[16,1,256]{2,1,0:T(1,128)} %stack.9), calls=%async_computation.3 | async-start | bytes 32768 | tf_op jit(solution)/shard_map/all_to_all | solution.py:109
  40.3 30.4 %collective-permute-start.9 = (f32[66,1]{1,0:T(8,128)S(1)}, f32[66,1]{1,0:T(8,128)S(1)}, u32[]{:S(2)}, u32[]{:S(2)}) collective-permute-start(f32[66,1]{1,0:T(8,128)S(1)} %get-tuple-element.101), channel_id=1, source_target_pairs={{1,0},{2,1},{3,2},{4,3},{5,4},{6,5},{7,6},{8,7},{9,8},{10,9},{11,1... | collective-permute-start | bytes 800 | tf_op jit(solution)/shard_map/ppermute | solution.py:26
  41.6 29.1 %collective-permute-start.8 = (f32[66,1]{1,0:T(8,128)S(1)}, f32[66,1]{1,0:T(8,128)S(1)}, u32[]{:S(2)}, u32[]{:S(2)}) collective-permute-start(f32[66,1]{1,0:T(8,128)S(1)} %get-tuple-element.100), channel_id=1, source_target_pairs={{0,1},{1,2},{2,3},{3,4},{4,5},{5,6},{6,7},{7,8},{8,9},{9,10},{10,1... | collective-permute-start | bytes 800 | tf_op jit(solution)/shard_map/ppermute | solution.py:23
  90.3 54.0 %collective-permute-start.15 = (f32[1,256]{1,0:T(1,128)S(1)}, f32[1,256]{1,0:T(1,128)S(1)}, u32[]{:S(2)}, u32[]{:S(2)}) collective-permute-start(f32[1,256]{1,0:T(1,128)S(1)} %get-tuple-element.121), channel_id=1, source_target_pairs={{16,0},{32,16},{48,32},{64,48},{80,64},{96,80},{112,96},{17,1},{33... | collective-permute-start | bytes 3080 | tf_op jit(solution)/shard_map/ppermute | solution.py:26
  92.2 52.0 %collective-permute-start.14 = (f32[1,256]{1,0:T(1,128)S(1)}, f32[1,256]{1,0:T(1,128)S(1)}, u32[]{:S(2)}, u32[]{:S(2)}) collective-permute-start(f32[1,256]{1,0:T(1,128)S(1)} %get-tuple-element.120), channel_id=1, source_target_pairs={{0,16},{16,32},{32,48},{48,64},{64,80},{80,96},{96,112},{1,17},{17... | collective-permute-start | bytes 3080 | tf_op jit(solution)/shard_map/ppermute | solution.py:23
  144.4 51.5 %collective-permute-start.17 = (f32[66,1]{1,0:T(8,128)S(1)}, f32[66,1]{1,0:T(8,128)S(1)}, u32[]{:S(2)}, u32[]{:S(2)}) collective-permute-start(f32[66,1]{1,0:T(8,128)S(1)} %get-tuple-element.97), channel_id=1, source_target_pairs={{1,0},{2,1},{3,2},{4,3},{5,4},{6,5},{7,6},{8,7},{9,8},{10,9},{11,1... | collective-permute-start | bytes 800 | tf_op jit(solution)/shard_map/ppermute | solution.py:26
  145.7 50.3 %collective-permute-start.16 = (f32[66,1]{1,0:T(8,128)S(1)}, f32[66,1]{1,0:T(8,128)S(1)}, u32[]{:S(2)}, u32[]{:S(2)}) collective-permute-start(f32[66,1]{1,0:T(8,128)S(1)} %get-tuple-element.96), channel_id=1, source_target_pairs={{0,1},{1,2},{2,3},{3,4},{4,5},{5,6},{6,7},{7,8},{8,9},{9,10},{10,1... | collective-permute-start | bytes 800 | tf_op jit(solution)/shard_map/ppermute | solution.py:23
  261.4 49.4 %all-to-all-start.1 = ((f32[128,1,64]{2,1,0:T(1,128)}), f32[128,1,64]{2,1,0:T(1,128)S(1)}, u32[]{:S(2)}, u32[]{:S(2)}) async-start(f32[128,1,64]{2,1,0:T(1,128)} %bitcast.5), calls=%async_computation.1 | async-start | bytes 131072 | tf_op jit(solution)/shard_map/all_to_all | solution.py:99
  402.6 33.3 %collective-permute-start.29 = (f32[66,1]{1,0:T(8,128)S(1)}, f32[66,1]{1,0:T(8,128)S(1)}, u32[]{:S(2)}, u32[]{:S(2)}) collective-permute-start(f32[66,1]{1,0:T(8,128)S(1)} %get-tuple-element.91), channel_id=1, source_target_pairs={{1,0},{2,1},{3,2},{4,3},{5,4},{6,5},{7,6},{8,7},{9,8},{10,9},{11,1... | collective-permute-start | bytes 800 | tf_op jit(solution)/shard_map/ppermute | solution.py:26
  403.8 32.0 %collective-permute-start.28 = (f32[66,1]{1,0:T(8,128)S(1)}, f32[66,1]{1,0:T(8,128)S(1)}, u32[]{:S(2)}, u32[]{:S(2)}) collective-permute-start(f32[66,1]{1,0:T(8,128)S(1)} %get-tuple-element.90), channel_id=1, source_target_pairs={{0,1},{1,2},{2,3},{3,4},{4,5},{5,6},{6,7},{7,8},{8,9},{9,10},{10,1... | collective-permute-start | bytes 800 | tf_op jit(solution)/shard_map/ppermute | solution.py:23
  436.0 62.2 %collective-permute-start.31 = (f32[1,256]{1,0:T(1,128)S(1)}, f32[1,256]{1,0:T(1,128)S(1)}, u32[]{:S(2)}, u32[]{:S(2)}) collective-permute-start(f32[1,256]{1,0:T(1,128)S(1)} %get-tuple-element.113), channel_id=1, source_target_pairs={{16,0},{32,16},{48,32},{64,48},{80,64},{96,80},{112,96},{17,1},{33... | collective-permute-start | bytes 3080 | tf_op jit(solution)/shard_map/ppermute | solution.py:26
  441.2 57.1 %collective-permute-start.30 = (f32[1,256]{1,0:T(1,128)S(1)}, f32[1,256]{1,0:T(1,128)S(1)}, u32[]{:S(2)}, u32[]{:S(2)}) collective-permute-start(f32[1,256]{1,0:T(1,128)S(1)} %get-tuple-element.112), channel_id=1, source_target_pairs={{0,16},{16,32},{32,48},{48,64},{64,80},{80,96},{96,112},{1,17},{17... | collective-permute-start | bytes 3080 | tf_op jit(solution)/shard_map/ppermute | solution.py:23
  552.9 20.6 %all-to-all-start.2 = ((f32[128,1,64]{2,1,0:T(1,128)}), f32[128,1,64]{2,1,0:T(1,128)S(1)}, u32[]{:S(2)}, u32[]{:S(2)}) async-start(f32[128,1,64]{2,1,0:T(1,128)} %bitcast.9), calls=%async_computation.2 | async-start | bytes 131072 | tf_op jit(solution)/shard_map/all_to_all | solution.py:94
  574.1 49.4 %all-to-all-start.4 = ((f32[128,1,64]{2,1,0:T(1,128)}), f32[128,1,64]{2,1,0:T(1,128)S(1)}, u32[]{:S(2)}, u32[]{:S(2)}) async-start(f32[128,1,64]{2,1,0:T(1,128)} %bitcast.24), calls=%async_computation.4 | async-start | bytes 131072 | tf_op jit(solution)/shard_map/all_to_all | solution.py:99
  715.2 33.3 %collective-permute-start.45 = (f32[66,1]{1,0:T(8,128)S(1)}, f32[66,1]{1,0:T(8,128)S(1)}, u32[]{:S(2)}, u32[]{:S(2)}) collective-permute-start(f32[66,1]{1,0:T(8,128)S(1)} %get-tuple-element.83), channel_id=1, source_target_pairs={{1,0},{2,1},{3,2},{4,3},{5,4},{6,5},{7,6},{8,7},{9,8},{10,9},{11,1... | collective-permute-start | bytes 800 | tf_op jit(solution)/shard_map/ppermute | solution.py:26
  716.5 32.0 %collective-permute-start.44 = (f32[66,1]{1,0:T(8,128)S(1)}, f32[66,1]{1,0:T(8,128)S(1)}, u32[]{:S(2)}, u32[]{:S(2)}) collective-permute-start(f32[66,1]{1,0:T(8,128)S(1)} %get-tuple-element.82), channel_id=1, source_target_pairs={{0,1},{1,2},{2,3},{3,4},{4,5},{5,6},{6,7},{7,8},{8,9},{9,10},{10,1... | collective-permute-start | bytes 800 | tf_op jit(solution)/shard_map/ppermute | solution.py:23
  748.7 62.2 %collective-permute-start.47 = (f32[1,256]{1,0:T(1,128)S(1)}, f32[1,256]{1,0:T(1,128)S(1)}, u32[]{:S(2)}, u32[]{:S(2)}) collective-permute-start(f32[1,256]{1,0:T(1,128)S(1)} %get-tuple-element.105), channel_id=1, source_target_pairs={{16,0},{32,16},{48,32},{64,48},{80,64},{96,80},{112,96},{17,1},{33... | collective-permute-start | bytes 3080 | tf_op jit(solution)/shard_map/ppermute | solution.py:26
  753.9 57.1 %collective-permute-start.46 = (f32[1,256]{1,0:T(1,128)S(1)}, f32[1,256]{1,0:T(1,128)S(1)}, u32[]{:S(2)}, u32[]{:S(2)}) collective-permute-start(f32[1,256]{1,0:T(1,128)S(1)} %get-tuple-element.104), channel_id=1, source_target_pairs={{0,16},{16,32},{32,48},{48,64},{64,80},{80,96},{96,112},{1,17},{17... | collective-permute-start | bytes 3080 | tf_op jit(solution)/shard_map/ppermute | solution.py:23
  865.5 20.6 %all-to-all-start.5 = ((f32[128,1,64]{2,1,0:T(1,128)}), f32[128,1,64]{2,1,0:T(1,128)S(1)}, u32[]{:S(2)}, u32[]{:S(2)}) async-start(f32[128,1,64]{2,1,0:T(1,128)} %bitcast.28), calls=%async_computation.5 | async-start | bytes 131072 | tf_op jit(solution)/shard_map/all_to_all | solution.py:94
  932.4 19.5 %all-to-all-start.7 = ((f32[128,1,64]{2,1,0:T(1,128)}), f32[128,1,64]{2,1,0:T(1,128)S(1)}, u32[]{:S(2)}, u32[]{:S(2)}) async-start(f32[128,1,64]{2,1,0:T(1,128)} %bitcast.37), calls=%async_computation.7 | async-start | bytes 131072 | tf_op jit(solution)/shard_map/all_to_all | solution.py:99
  (48 other events, 362.5 us)
